TPU v7x, 32 devices: a whole 2x2x4 slice. The times are simulated.
32 devices in a mesh: section: 4 (over x, core), blk: 4 (over z), tp: 2 (over y).
Axes of the slice: x: 2, y: 2, z: 4, core: 2. Of those that a mesh axis runs over, the one named last changes fastest.
Arguments:
- query: bfloat16 [2048, 8192], P(('section', 'blk'), 'tp'), may hold values from -6 to 6
- text_frame: int32 [2048], P(('section', 'blk')), may hold values from 0 to 63
- image_feats: bfloat16 [1024, 8192], P('blk', ('section', 'tp')), may hold values from -6 to 6
- image_frame: int32 [1024], P('blk'), may hold values from 0 to 63, never falling along the last dimension, each value on 1 to 32 neighbouring positions
- kv_weight: bfloat16 [4, 8192, 2, 1024], P('section', None, None, 'tp'), may hold values from -0.0625 to 0.0625
- query_gain: float32 [4, 128], P('section'), may hold values from 0.1 to 1.9
- key_gain: float32 [4, 128], P('section'), may hold values from 0.1 to 1.9
Outputs:
- attended: bfloat16 [2048, 8192], P(('section', 'blk'), 'tp')
Inputs may be any that keep to these rules, and one draw needn't show every extreme that they name: `image_frame`: image frame ids never fall along the image tokens; every frame has at least one token.
All inputs are finite; a program needn't handle non-finite values.
Results may differ from a plain program's by a relative error of at most 0.007.
Values may be sent and summed in bfloat16 or wider, within the bound.
A program may use at most 128 MiB of HBM per device.

v0:
```python
import jax
import jax.numpy as jnp
from jax import lax
from jax.sharding import PartitionSpec as P


def normalize(x):
    return x * lax.rsqrt(jnp.mean(x * x, axis=-1, keepdims=True) + 1e-05)


def per_device(query, text_frame, image_feats, image_frame, kv_weight, query_gain, key_gain):
    head_size = query_gain.shape[1]
    feat_width = kv_weight.shape[1]
    kv_cols = kv_weight.shape[3]
    heads_kv = kv_cols // head_size
    text_rows = query.shape[0]
    groups = query.shape[1] // kv_cols
    block_rows = image_feats.shape[0]
    weight_flat = kv_weight[0].reshape(feat_width, 2 * kv_cols)
    wide = lax.all_gather(image_feats, ("section", "tp"), axis=1, tiled=True)
    proj = jnp.dot(wide, weight_flat, preferred_element_type=jnp.float32)
    proj = proj.reshape(block_rows, 2, heads_kv, head_size)
    keys = (normalize(proj[:, 0]) * key_gain[0]).astype(jnp.bfloat16)
    values = proj[:, 1].astype(jnp.bfloat16)
    key_value = jnp.stack([keys, values], axis=1).reshape(block_rows, 2, kv_cols)
    qrows = query.astype(jnp.float32).reshape(text_rows, heads_kv, groups, head_size)
    qn = (normalize(qrows) * query_gain[0] * head_size ** (-0.5)).astype(jnp.bfloat16)
    block = lax.all_gather(key_value, "blk", axis=0, tiled=True)
    frames = lax.all_gather(image_frame, "blk", axis=0, tiled=True)
    count = block.shape[0]
    keys_part = block[:, 0].reshape(count, heads_kv, head_size)
    values_part = block[:, 1].reshape(count, heads_kv, head_size)
    scores = jnp.einsum("tkgd,skd->kgts", qn, keys_part, preferred_element_type=jnp.float32)
    allowed = frames[None, :] <= text_frame[:, None]
    weights = jnp.where(allowed, jnp.exp(scores), jnp.float32(0.0))
    total = jnp.sum(weights, axis=-1)
    wb = weights.astype(jnp.bfloat16)
    summed = jnp.einsum("kgts,skd->kgtd", wb, values_part, preferred_element_type=jnp.float32)
    result = summed / total[..., None]
    return (
        result.transpose(2, 0, 1, 3)
        .reshape(text_rows, heads_kv * groups * head_size)
        .astype(jnp.bfloat16)
    )


def solution(mesh):
    return jax.shard_map(
        per_device,
        mesh=mesh,
        in_specs=(
            P(("section", "blk"), "tp"),
            P(("section", "blk")),
            P("blk", ("section", "tp")),
            P("blk"),
            P("section", None, None, "tp"),
            P("section", None),
            P("section", None),
        ),
        out_specs=P(("section", "blk"), "tp"),
        check_vma=False,
    )
```

profile of v0, /device:TPU:0, one launch (start us, length us, event | category | flops | bytes accessed | tf_op | source)
XLA Modules:
  0.0 122.1 jit_solution(2899087948636825844)
XLA Ops:
  6.5 0.0 all-gather.4.cloned.1.call-start
  6.5 0.7 all-gather.4.cloned.1.call-update
  7.3 0.0 all-gather.6.cloned.1.call-start
  7.3 16.7 %copy.35 = bf16[1024,8,2,512]{3,1,2,0:T(8,128)(2,1)} copy(bf16[1024,8,2,512]{3,2,1,0:T(2,128)(2,1)} %bitcast.52) | data formatting | bytes 33554432
  24.0 21.3 %copy.22 = bf16[1024,8192]{1,0:T(8,128)(2,1)} copy(bf16[1024,8192]{0,1:T(8,128)(2,1)} %bitcast.49) | data formatting | bytes 33554432 | tf_op jit(solution)/shard_map/dot_general | solution.py:21
  45.3 3.4 %all-gather.4.cloned.1.call-done = bf16[256,8192]{1,0:T(8,128)(2,1)} async-done(((bf16[256,1024]{1,0:T(8,128)(2,1)}), bf16[256,8192]{1,0:T(8,128)(2,1)}) %all-gather.4.cloned.1.call-update) | async-done | bytes 4194320 | tf_op jit(solution)/shard_map/all_gather | solution.py:20
  48.7 0.0 copy-start.4
  48.7 0.0 copy-start
  48.7 9.4 %fusion.6 = f32[256,2,4,128]{0,3,2,1:T(8,128)S(1)} fusion(bf16[2,4,128,8192]{3,2,1,0:T(8,128)(2,1)} %bitcast.53, bf16[256,8192]{1,0:T(8,128)(2,1)} %all-gather.4.cloned.1.call-done), kind=kOutput, calls=%fused_computation.6 | convolution fusion | flops 4294967296 | bytes 22020096 | tf_op jit(solution)/shard_map/dot_general | solution.py:21
  58.2 0.1 multiply_reduce_fusion.1
  58.3 0.0 copy-done.4
  58.3 0.1 multiply_convert_fusion.1
  58.4 0.8 pad_maximum_fusion
  59.2 0.0 all-gather.6.cloned.1.call-update
  59.2 0.0 copy-done
  59.2 0.2 convert_bitcast_fusion
  59.5 0.0 copy-start.1
  59.5 0.0 copy-start.2
  59.5 0.0 copy-start.3
  59.5 0.4 copy.36
  59.9 0.8 multiply_reduce_fusion
  60.7 0.1 copy.23
  60.8 0.2 copy.24
  61.0 0.0 copy-done.1
  61.0 11.0 %all-gather = s32[4,1,256]{2,1,0:T(1,128)S(1)} all-gather(s32[1,1,256]{2,1,0:T(1,128)S(1)} %bitcast.61), channel_id=1, replica_groups=mesh['section'=4,'blk'=4,'tp'=2] {'blk'}, dimensions={0}, use_global_device_ids=true | all-gather | bytes 5120 | tf_op jit(solution)/shard_map/all_gather | solution.py:29
  72.0 0.0 copy-done.2
  72.0 0.2 broadcast_compare_fusion
  72.2 0.0 copy-done.3
  72.2 0.7 multiply_convert_fusion
  73.0 32.7 %all-gather.6.cloned.1.call-done = bf16[1024,2,512]{0,2,1:T(8,128)(2,1)} async-done(((bf16[256,2,512]{0,2,1:T(8,128)(2,1)}), bf16[1024,2,512]{0,2,1:T(8,128)(2,1)}) %all-gather.6.cloned.1.call-update) | async-done | bytes 2097168 | tf_op jit(solution)/shard_map/all_gather | solution.py:28
  105.6 1.7 %fusion.14 = (bf16[1024,1,512]{0,2,1:T(8,128)(2,1)S(1)}, bf16[1024,1,512]{0,2,1:T(8,128)(2,1)S(1)}) fusion(bf16[1024,2,512]{0,2,1:T(8,128)(2,1)} %all-gather.6.cloned.1.call-done), kind=kLoop, calls=%fused_computation.23 | loop fusion | bytes 4194304 | tf_op jit(solution)/shard_map/slice | solution.py:31
  107.4 3.4 %fusion = (f32[4,8,128]{2,1,0:T(8,128)S(1)}, f32[4,1024,128,8]{2,1,3,0:T(8,128)S(1)}) fusion(pred[128,1024]{0,1:T(8,128)(4,1)S(1)} %broadcast_compare_fusion, bf16[1024,4,128,1]{0,2,3,1:T(8,128)(2,1)S(1)} %bitcast.54, bf16[128,4,8,128]{3,2,1,0:T(8,128)(2,1)S(1)} %multiply_convert_fusion), kind=kOutput, calls=%fused_computation.1 | convolution fusion | flops 1082126336 | bytes 19021824 | tf_op jit(solution)/shard_map/tkgd,skd->kgts/dot_general | solution.py:33
  110.8 3.2 %fusion.8 = bf16[128,4,8,128]{0,3,2,1:T(8,128)(2,1)S(1)} fusion(bf16[1024,4,128,1]{0,2,3,1:T(8,128)(2,1)S(1)} %bitcast.57, f32[4,1024,128,8]{2,1,3,0:T(8,128)S(1)} %get-tuple-element.8, pred[128,1024]{0,1:T(8,128)(4,1)S(1)} %broadcast_compare_fusion, f32[128,4,8]{0,2,1:T(8,128)S(1)} %bitcast.60), kind=kOutput, calls=%fused_computation.9 | convolution fusion | flops 1083179008 | bytes 19021824 | tf_op jit(solution)/shard_map/kgts,skd->kgtd/dot_general | solution.py:38
  114.0 1.3 %copy.28 = bf16[128,4096]{1,0:T(8,128)(2,1)} copy(bf16[128,4096]{0,1:T(8,128)(2,1)S(1)} %bitcast.55) | data formatting | bytes 2097152 | tf_op jit(solution)/shard_map/convert_element_type | solution.py:43
  (3 shorter events, 0.0 us)
Async XLA Ops:
  6.5 42.2 %all-gather.4.cloned.1.call-start = ((), (), s32[]{:S(2)}) async-start(), calls=%async_computation | async-start | bytes 4718592 | tf_op jit(solution)/shard_map/all_gather | solution.py:20
  7.3 98.4 %all-gather.6.cloned.1.call-start = ((), (), s32[]{:S(2)}) async-start(), calls=%async_computation.1 | async-start | bytes 2621440 | tf_op jit(solution)/shard_map/all_gather | solution.py:28
  48.7 9.6 %copy-start.4 = (f32[1,128]{1,0:T(1,128)S(1)}, f32[1,128]{1,0:T(1,128)}, u32[]{:S(2)}) copy-start(f32[1,128]{1,0:T(1,128)} %param.13) | copy-start | bytes 1540
  48.7 10.5 %copy-start = (bf16[128,4096]{1,0:T(8,128)(2,1)S(1)}, bf16[128,4096]{1,0:T(8,128)(2,1)}, u32[]{:S(2)}) copy-start(bf16[128,4096]{1,0:T(8,128)(2,1)} %param.7) | copy-start | bytes 3145732
  59.5 1.5 %copy-start.1 = (s32[256]{0:T(256)S(1)}, s32[256]{0:T(256)}, u32[]{:S(2)}) copy-start(s32[256]{0:T(256)} %param.10) | copy-start | bytes 3076
  59.5 12.5 %copy-start.2 = (s32[128]{0:T(128)S(1)}, s32[128]{0:T(128)}, u32[]{:S(2)}) copy-start(s32[128]{0:T(128)} %param.8) | copy-start | bytes 1540
  59.5 12.7 %copy-start.3 = (f32[1,128]{1,0:T(1,128)S(1)}, f32[1,128]{1,0:T(1,128)}, u32[]{:S(2)}) copy-start(f32[1,128]{1,0:T(1,128)} %param.12) | copy-start | bytes 1540
Sparse Core Ops, SparseCore 0:
  9.3 39.4 all-gather.3
  59.4 46.2 all-gather.5
where the time goes:
time: 123 us; the launch traced here: 122 us
  local copies, waits for them, and re-layouts  41.7 us (34%)
  waiting for transfers between devices  36.8 us (30%)
  matrix products  16 us (13%)
  between operations  13.6 us (11%)
  blocking collectives  11 us (9%)
  other arithmetic  2.98 us (2%)
    all_gather x1, waiting for transfers between devices, per_device(): block = lax.all_gather(key_value, 'blk', axis=0, tiled=True)  32.7 us
    dot_general x1, local copies, waits for them, and re-layouts, per_device(): proj = jnp.dot(wide, weight_flat, preferred_element_type=jnp.float32)  21.3 us
    unnamed x12, local copies, waits for them, and re-layouts  17.1 us
    all_gather x1, blocking collectives, per_device(): frames = lax.all_gather(image_frame, 'blk', axis=0, tiled=True)  11 us
    dot_general x1, matrix products, per_device(): proj = jnp.dot(wide, weight_flat, preferred_element_type=jnp.float32)  9.44 us
    dot_general x1, matrix products, per_device(): jnp.einsum('tkgd,skd->kgts', qn, keys_part, preferred_element_type=jnp.fl...  3.4 us
    all_gather x1, waiting for transfers between devices, per_device(): wide = lax.all_gather(image_feats, ('section', 'tp'), axis=1, tiled=True)  3.39 us
    dot_general x1, matrix products, per_device(): jnp.einsum('kgts,skd->kgtd', wb, values_part, preferred_element_type=jnp....  3.22 us
  transfers between devices with their start and end apart: 2, of which 2 were waited for; matrix products, arithmetic and copies ran while one was open for 33% of the time, Pallas kernels for 0%

commit v1 on v0

--- a/solution.py
+++ b/solution.py
@@ -26,7 +26,21 @@
     qrows = query.astype(jnp.float32).reshape(text_rows, heads_kv, groups, head_size)
     qn = (normalize(qrows) * query_gain[0] * head_size ** (-0.5)).astype(jnp.bfloat16)
     block = lax.all_gather(key_value, "blk", axis=0, tiled=True)
-    frames = lax.all_gather(image_frame, "blk", axis=0, tiled=True)
+    fields = [image_frame]
+    p_count = lax.axis_size("blk")
+    for k in range(p_count - 1):
+        fields.append(
+            lax.ppermute(
+                fields[-1],
+                axis_name="blk",
+                perm=[(i0, (i0 + 1) % p_count) for i0 in range(p_count)],
+            )
+        )
+    frames = jnp.roll(
+        jnp.concatenate(fields[::-1], axis=0),
+        (lax.axis_index("blk") + 1) * image_frame.shape[0],
+        axis=0,
+    )
     count = block.shape[0]
     keys_part = block[:, 0].reshape(count, heads_kv, head_size)
     values_part = block[:, 1].reshape(count, heads_kv, head_size)

time: 123 us -> 123 us (level)
  blocking collectives: 11 us -> 0 us
  waiting for transfers between devices: 36.8 us -> 46.3 us
  starting transfers between devices: 0.04 us -> 1.58 us
    ppermute x0 -> x3, waiting for transfers between devices: none -> 12.2 us  [per_device(): lax.ppermute(fields[-1], axis_name='blk', perm=[(i0, (i0 + 1) % p_count)...]
    all_gather x1 -> x0, blocking collectives: 11 us -> none  [per_device(): frames = lax.all_gather(image_frame, 'blk', axis=0, tiled=True)]
    all_gather x1, waiting for transfers between devices: 32.7 us -> 29.8 us  [per_device(): block = lax.all_gather(key_value, 'blk', axis=0, tiled=True)]
    ppermute x0 -> x3, starting transfers between devices: none -> 1.54 us  [per_device(): lax.ppermute(fields[-1], axis_name='blk', perm=[(i0, (i0 + 1) % p_count)...]
    unnamed x12 -> x19, local copies, waits for them, and re-layouts: 17.1 us -> 17.1 us
  transfers between devices with their start and end apart: 2 -> 5, of which waited for: 2 -> 5; matrix products, arithmetic and copies ran while one was open for 33% -> 33% of each run, Pallas kernels for 0% -> 0%
where the time goes in v1:
time: 123 us; the launch traced here: 122 us
  waiting for transfers between devices  46.3 us (38%)
  local copies, waits for them, and re-layouts  41.7 us (34%)
  matrix products  16.2 us (13%)
  between operations  13.6 us (11%)
  other arithmetic  2.94 us (2%)
  starting transfers between devices  1.58 us (1%)
    all_gather x1, waiting for transfers between devices, per_device(): block = lax.all_gather(key_value, 'blk', axis=0, tiled=True)  29.8 us
    dot_general x1, local copies, waits for them, and re-layouts, per_device(): proj = jnp.dot(wide, weight_flat, preferred_element_type=jnp.float32)  21.2 us
    unnamed x19, local copies, waits for them, and re-layouts  17.1 us
    ppermute x3, waiting for transfers between devices, per_device(): lax.ppermute(fields[-1], axis_name='blk', perm=[(i0, (i0 + 1) % p_count)...  12.2 us
    dot_general x1, matrix products, per_device(): proj = jnp.dot(wide, weight_flat, preferred_element_type=jnp.float32)  9.44 us
    all_gather x1, waiting for transfers between devices, per_device(): wide = lax.all_gather(image_feats, ('section', 'tp'), axis=1, tiled=True)  3.52 us
    dot_general x1, matrix products, per_device(): jnp.einsum('tkgd,skd->kgts', qn, keys_part, preferred_element_type=jnp.fl...  3.48 us
    dot_general x1, matrix products, per_device(): jnp.einsum('kgts,skd->kgtd', wb, values_part, preferred_element_type=jnp....  3.29 us
  transfers between devices with their start and end apart: 5, of which 5 were waited for; matrix products, arithmetic and copies ran while one was open for 33% of the time, Pallas kernels for 0%

profile of v1, /device:TPU:0, one launch (start us, length us, event | category | flops | bytes accessed | tf_op | source)
XLA Modules:
  0.0 122.3 jit_solution(9378162278102118457)
XLA Ops:
  6.5 0.0 all-gather.3.cloned.1.call-start
  6.5 0.7 all-gather.3.cloned.1.call-update
  7.3 0.0 all-gather.5.cloned.1.call-start
  7.3 16.7 %copy.35 = bf16[1024,8,2,512]{3,1,2,0:T(8,128)(2,1)} copy(bf16[1024,8,2,512]{3,2,1,0:T(2,128)(2,1)} %bitcast.50) | data formatting | bytes 33554432
  24.0 21.2 %copy.22 = bf16[1024,8192]{1,0:T(8,128)(2,1)} copy(bf16[1024,8192]{0,1:T(8,128)(2,1)} %bitcast.47) | data formatting | bytes 33554432 | tf_op jit(solution)/shard_map/dot_general | solution.py:21
  45.2 3.5 %all-gather.3.cloned.1.call-done = bf16[256,8192]{1,0:T(8,128)(2,1)} async-done(((bf16[256,1024]{1,0:T(8,128)(2,1)}), bf16[256,8192]{1,0:T(8,128)(2,1)}) %all-gather.3.cloned.1.call-update) | async-done | bytes 4194320 | tf_op jit(solution)/shard_map/all_gather | solution.py:20
  48.7 0.0 copy-start.4
  48.7 0.0 copy-start.1
  48.7 0.0 copy-start
  48.7 9.4 %fusion.6 = f32[256,2,4,128]{0,3,2,1:T(8,128)S(1)} fusion(bf16[2,4,128,8192]{3,2,1,0:T(8,128)(2,1)} %bitcast.51, bf16[256,8192]{1,0:T(8,128)(2,1)} %all-gather.3.cloned.1.call-done), kind=kOutput, calls=%fused_computation.6 | convolution fusion | flops 4294967296 | bytes 22020096 | tf_op jit(solution)/shard_map/dot_general | solution.py:21
  58.2 0.1 multiply_reduce_fusion.1
  58.3 0.0 copy-done.4
  58.3 0.1 multiply_convert_fusion.1
  58.4 0.8 pad_maximum_fusion
  59.2 0.0 all-gather.5.cloned.1.call-update
  59.2 0.0 copy-done.1
  59.3 1.5 %collective-permute-start = (s32[256]{0:T(256)S(1)}, s32[256]{0:T(256)S(1)}, u32[]{:S(2)}, u32[]{:S(2)}) collective-permute-start(s32[256]{0:T(256)S(1)} %copy-done.1), channel_id=1, source_target_pairs={{0,2},{2,4},{4,6},{6,0},{1,3},{3,5},{5,7},{7,1},{8,10},{10,12},{12... | collective-permute-start | bytes 3080 | tf_op jit(solution)/shard_map/ppermute | solution.py:33
  60.8 0.0 copy-done
  60.8 0.2 convert_bitcast_fusion
  61.0 0.0 copy-start.2
  61.0 0.4 copy.36
  61.4 0.0 copy-start.3
  61.4 0.8 multiply_reduce_fusion
  62.2 0.1 copy.23
  62.3 0.2 copy.24
  62.5 2.2 %collective-permute-done = s32[256]{0:T(256)S(1)} collective-permute-done((s32[256]{0:T(256)S(1)}, s32[256]{0:T(256)S(1)}, u32[]{:S(2)}, u32[]{:S(2)}) %collective-permute-start) | collective-permute-done | bytes 1056 | tf_op jit(solution)/shard_map/ppermute | solution.py:33
  64.7 0.0 collective-permute-start.1
  64.7 0.0 copy-done.2
  64.7 0.7 multiply_convert_fusion
  65.4 4.6 %collective-permute-done.1 = s32[256]{0:T(256)S(1)} collective-permute-done((s32[256]{0:T(256)S(1)}, s32[256]{0:T(256)S(1)}, u32[]{:S(2)}, u32[]{:S(2)}) %collective-permute-start.1) | collective-permute-done | bytes 1056 | tf_op jit(solution)/shard_map/ppermute | solution.py:33
  70.0 0.0 collective-permute-start.2
  70.0 5.4 %collective-permute-done.2 = s32[256]{0:T(256)S(1)} collective-permute-done((s32[256]{0:T(256)S(1)}, s32[256]{0:T(256)S(1)}, u32[]{:S(2)}, u32[]{:S(2)}) %collective-permute-start.2) | collective-permute-done | bytes 1056 | tf_op jit(solution)/shard_map/ppermute | solution.py:33
  75.6 0.1 dynamic_slice.4
  75.6 0.0 copy-done.3
  75.7 0.2 broadcast_compare_fusion
  75.9 29.8 %all-gather.5.cloned.1.call-done = bf16[1024,2,512]{0,2,1:T(8,128)(2,1)} async-done(((bf16[256,2,512]{0,2,1:T(8,128)(2,1)}), bf16[1024,2,512]{0,2,1:T(8,128)(2,1)}) %all-gather.5.cloned.1.call-update) | async-done | bytes 2097168 | tf_op jit(solution)/shard_map/all_gather | solution.py:28
  105.7 1.7 %fusion.14 = (bf16[1024,1,512]{0,2,1:T(8,128)(2,1)S(1)}, bf16[1024,1,512]{0,2,1:T(8,128)(2,1)S(1)}) fusion(bf16[1024,2,512]{0,2,1:T(8,128)(2,1)} %all-gather.5.cloned.1.call-done), kind=kLoop, calls=%fused_computation.31 | loop fusion | bytes 4194304 | tf_op jit(solution)/shard_map/slice | solution.py:45
  107.4 3.5 %fusion = (f32[4,8,128]{2,1,0:T(8,128)S(1)}, f32[4,1024,128,8]{2,1,3,0:T(8,128)S(1)}) fusion(pred[128,1024]{0,1:T(8,128)(4,1)S(1)} %broadcast_compare_fusion, bf16[1024,4,128,1]{0,2,3,1:T(8,128)(2,1)S(1)} %bitcast.52, bf16[128,4,8,128]{3,2,1,0:T(8,128)(2,1)S(1)} %multiply_convert_fusion), kind=kOutput, calls=%fused_computation.1 | convolution fusion | flops 1082126336 | bytes 19021824 | tf_op jit(solution)/shard_map/tkgd,skd->kgts/dot_general | solution.py:47
  110.9 3.3 %fusion.8 = bf16[128,4,8,128]{0,3,2,1:T(8,128)(2,1)S(1)} fusion(bf16[1024,4,128,1]{0,2,3,1:T(8,128)(2,1)S(1)} %bitcast.55, f32[4,1024,128,8]{2,1,3,0:T(8,128)S(1)} %get-tuple-element.8, pred[128,1024]{0,1:T(8,128)(4,1)S(1)} %broadcast_compare_fusion, f32[128,4,8]{0,2,1:T(8,128)S(1)} %bitcast.57), kind=kOutput, calls=%fused_computation.9 | convolution fusion | flops 1083179008 | bytes 19021824 | tf_op jit(solution)/shard_map/kgts,skd->kgtd/dot_general | solution.py:52
  114.2 1.3 %copy.28 = bf16[128,4096]{1,0:T(8,128)(2,1)} copy(bf16[128,4096]{0,1:T(8,128)(2,1)S(1)} %bitcast.53) | data formatting | bytes 2097152 | tf_op jit(solution)/shard_map/convert_element_type | solution.py:57
  (12 shorter events, 0.1 us)
Async XLA Ops:
  6.5 42.2 %all-gather.3.cloned.1.call-start = ((), (), s32[]{:S(2)}) async-start(), calls=%async_computation | async-start | bytes 4718592 | tf_op jit(solution)/shard_map/all_gather | solution.py:20
  7.3 98.4 %all-gather.5.cloned.1.call-start = ((), (), s32[]{:S(2)}) async-start(), calls=%async_computation.1 | async-start | bytes 2621440 | tf_op jit(solution)/shard_map/all_gather | solution.py:28
  48.7 9.6 %copy-start.4 = (f32[1,128]{1,0:T(1,128)S(1)}, f32[1,128]{1,0:T(1,128)}, u32[]{:S(2)}) copy-start(f32[1,128]{1,0:T(1,128)} %param.13) | copy-start | bytes 1540
  48.7 10.5 %copy-start.1 = (s32[256]{0:T(256)S(1)}, s32[256]{0:T(256)}, u32[]{:S(2)}) copy-start(s32[256]{0:T(256)} %param.10) | copy-start | bytes 3076
  48.7 12.1 %copy-start = (bf16[128,4096]{1,0:T(8,128)(2,1)S(1)}, bf16[128,4096]{1,0:T(8,128)(2,1)}, u32[]{:S(2)}) copy-start(bf16[128,4096]{1,0:T(8,128)(2,1)} %param.7) | copy-start | bytes 3145732
  59.3 5.4 %collective-permute-start = (s32[256]{0:T(256)S(1)}, s32[256]{0:T(256)S(1)}, u32[]{:S(2)}, u32[]{:S(2)}) collective-permute-start(s32[256]{0:T(256)S(1)} %copy-done.1), channel_id=1, source_target_pairs={{0,2},{2,4},{4,6},{6,0},{1,3},{3,5},{5,7},{7,1},{8,10},{10,12},{12... | collective-permute-start | bytes 3080 | tf_op jit(solution)/shard_map/ppermute | solution.py:33
  61.0 3.7 %copy-start.2 = (f32[1,128]{1,0:T(1,128)S(1)}, f32[1,128]{1,0:T(1,128)}, u32[]{:S(2)}) copy-start(f32[1,128]{1,0:T(1,128)} %param.12) | copy-start | bytes 1540
  61.4 14.3 %copy-start.3 = (s32[128]{0:T(128)S(1)}, s32[128]{0:T(128)}, u32[]{:S(2)}) copy-start(s32[128]{0:T(128)} %param.8) | copy-start | bytes 1540
  64.7 5.4 %collective-permute-start.1 = (s32[256]{0:T(256)S(1)}, s32[256]{0:T(256)S(1)}, u32[]{:S(2)}, u32[]{:S(2)}) collective-permute-start(s32[256]{0:T(256)S(1)} %collective-permute-done), channel_id=1, source_target_pairs={{0,2},{2,4},{4,6},{6,0},{1,3},{3,5},{5,7},{7,1},{8,10},{10,12},{12... | collective-permute-start | bytes 3080 | tf_op jit(solution)/shard_map/ppermute | solution.py:33
  70.0 5.4 %collective-permute-start.2 = (s32[256]{0:T(256)S(1)}, s32[256]{0:T(256)S(1)}, u32[]{:S(2)}, u32[]{:S(2)}) collective-permute-start(s32[256]{0:T(256)S(1)} %collective-permute-done.1), channel_id=1, source_target_pairs={{0,2},{2,4},{4,6},{6,0},{1,3},{3,5},{5,7},{7,1},{8,10},{10,12},{12... | collective-permute-start | bytes 3080 | tf_op jit(solution)/shard_map/ppermute | solution.py:33
Sparse Core Ops, SparseCore 0:
  9.3 39.4 all-gather.2
  59.4 46.2 all-gather.4
